TPU v7x, 32 devices: a whole 2x2x4 slice. The times are simulated.
32 devices in a mesh: seq: 16 (over z, y, x), batch: 2 (over core).
Axes of the slice: x: 2, y: 2, z: 4, core: 2. Of those that a mesh axis runs over, the one named last changes fastest.
Arguments:
- tokens: bfloat16 [2, 2048, 768], P('batch', 'seq'), may hold values from -6 to 6
- cotangent: bfloat16 [2, 2048, 768], P('batch', 'seq'), may hold values from -6 to 6
- prefix_len: int32 [2], P('batch'), may hold values from 204 to 1024
- gain_one: bfloat16 [768], P(('seq', 'batch')), may hold values from 0.25 to 1.75
- shift_one: bfloat16 [768], P(('seq', 'batch')), may hold values from -1.75 to 1.75
- w_query: bfloat16 [768, 768], P(('seq', 'batch')), may hold values from -0.21875 to 0.21875
- b_query: bfloat16 [768], P(('seq', 'batch')), may hold values from -3 to 3
- w_key: bfloat16 [768, 768], P(('seq', 'batch')), may hold values from -0.21875 to 0.21875
- w_value: bfloat16 [768, 768], P(('seq', 'batch')), may hold values from -0.21875 to 0.21875
- b_value: bfloat16 [768], P(('seq', 'batch')), may hold values from -3 to 3
- w_output: bfloat16 [768, 768], P(('seq', 'batch')), may hold values from -3.5 to 3.5
- b_output: bfloat16 [768], P(('seq', 'batch')), may hold values from -1.75 to 1.75
- gain_two: bfloat16 [768], P(('seq', 'batch')), may hold values from 0.25 to 1.75
- shift_two: bfloat16 [768], P(('seq', 'batch')), may hold values from -1.75 to 1.75
- w_up: bfloat16 [768, 3072], P(('seq', 'batch')), may hold values from -0.21875 to 0.21875
- b_up: bfloat16 [3072], P(('seq', 'batch')), may hold values from -3 to 3
- w_down: bfloat16 [3072, 768], P(('seq', 'batch')), may hold values from -0.109375 to 0.109375
- b_down: bfloat16 [768], P(('seq', 'batch')), may hold values from -1.75 to 1.75
Outputs:
- layer_out: bfloat16 [2, 2048, 768], P('batch', 'seq')
- grad_tokens: float32 [2, 2048, 768], P('batch', 'seq')
- grad_gain_one: float32 [768], P(('seq', 'batch'))
- grad_shift_one: float32 [768], P(('seq', 'batch'))
- grad_w_query: float32 [768, 768], P(('seq', 'batch'))
- grad_b_query: float32 [768], P(('seq', 'batch'))
- grad_w_key: float32 [768, 768], P(('seq', 'batch'))
- grad_w_value: float32 [768, 768], P(('seq', 'batch'))
- grad_b_value: float32 [768], P(('seq', 'batch'))
- grad_w_output: float32 [768, 768], P(('seq', 'batch'))
- grad_b_output: float32 [768], P(('seq', 'batch'))
- grad_gain_two: float32 [768], P(('seq', 'batch'))
- grad_shift_two: float32 [768], P(('seq', 'batch'))
- grad_w_up: float32 [768, 3072], P(('seq', 'batch'))
- grad_b_up: float32 [3072], P(('seq', 'batch'))
- grad_w_down: float32 [3072, 768], P(('seq', 'batch'))
- grad_b_down: float32 [768], P(('seq', 'batch'))
Inputs may be any that keep to these rules, and one draw needn't show every extreme that they name: `prefix_len`: one prefix length per sequence.
All inputs are finite; a program needn't handle non-finite values.
Results may differ from a plain program's by a relative error of at most 0.014.
Values may be sent and summed in bfloat16 or wider, within the bound.
No kernel may reach another device: no remote copies, remote signals or barrier semaphores. Data moves between devices by JAX's collectives and lax.ppermute only.
A program may use at most 192 MiB of HBM per device.

v0:
```python
import jax
import jax.numpy as jnp
from jax import lax
from jax.sharding import PartitionSpec as P

HD = 64
EPS = 1e-05


def normalize(values):
    centre = jnp.mean(values, axis=-1, keepdims=True)
    centred = values - centre
    spread = jnp.mean(centred * centred, axis=-1, keepdims=True)
    factor = lax.rsqrt(spread + EPS)
    return (centred * factor, factor)


def norm_backward(grad_out, normed, factor, gain):
    grad_gain = jnp.sum(grad_out * normed, axis=0)
    grad_shift = jnp.sum(grad_out, axis=0)
    scaled = grad_out * gain.astype(jnp.float32)
    grad_in = factor * (
        scaled
        - jnp.mean(scaled, axis=-1, keepdims=True)
        - normed * jnp.mean(scaled * normed, axis=-1, keepdims=True)
    )
    return (grad_in, grad_gain, grad_shift)


def over_rows(left, right):
    return lax.dot_general(
        left, right, (((0,), (0,)), ((), ())), preferred_element_type=jnp.float32
    )


def over_cols(left, right):
    return lax.dot_general(
        left, right, (((1,), (1,)), ((), ())), preferred_element_type=jnp.float32
    )


def pair_scores(q_part, k_part, row_ids, col_ids, prefix):
    scores = jnp.einsum("qhd,khd->hqk", q_part, k_part, preferred_element_type=jnp.float32) * 0.125
    allowed = (col_ids[None, :] <= row_ids[:, None]) | (col_ids[None, :] < prefix)
    return (jnp.where(allowed[None], scores, -1e30), allowed)


def grad_terms(q_part, do_part, lse_part, delta_part, k_part, v_part, row_ids, col_ids, prefix):
    scores, allowed = pair_scores(q_part, k_part, row_ids, col_ids, prefix)
    attn_prob = jnp.where(allowed[None], jnp.exp(scores - lse_part[:, :, None]), 0.0)
    prob_low = attn_prob.astype(jnp.bfloat16)
    d_prob = jnp.einsum("qhd,khd->hqk", do_part, v_part, preferred_element_type=jnp.float32)
    d_score = (attn_prob * (d_prob - delta_part[:, :, None])).astype(jnp.bfloat16)
    return (prob_low, d_score)


def body(
    tokens,
    cotangent,
    prefix_len,
    gain_one,
    shift_one,
    w_query,
    b_query,
    w_key,
    w_value,
    b_value,
    w_output,
    b_output,
    gain_two,
    shift_two,
    w_up,
    b_up,
    w_down,
    b_down,
):
    shards = (
        gain_one,
        shift_one,
        w_query,
        b_query,
        w_key,
        w_value,
        b_value,
        w_output,
        b_output,
        gain_two,
        shift_two,
        w_up,
        b_up,
        w_down,
        b_down,
    )
    gathered = (
        lax.all_gather(shards[0], ("seq", "batch"), axis=0, tiled=True),
        lax.all_gather(shards[1], ("seq", "batch"), axis=0, tiled=True),
        lax.all_gather(shards[2], ("seq", "batch"), axis=0, tiled=True),
        lax.all_gather(shards[3], ("seq", "batch"), axis=0, tiled=True),
        lax.all_gather(shards[4], ("seq", "batch"), axis=0, tiled=True),
        lax.all_gather(shards[5], ("seq", "batch"), axis=0, tiled=True),
        lax.all_gather(shards[6], ("seq", "batch"), axis=0, tiled=True),
        lax.all_gather(shards[7], ("seq", "batch"), axis=0, tiled=True),
        lax.all_gather(shards[8], ("seq", "batch"), axis=0, tiled=True),
        lax.all_gather(shards[9], ("seq", "batch"), axis=0, tiled=True),
        lax.all_gather(shards[10], ("seq", "batch"), axis=0, tiled=True),
        lax.all_gather(shards[11], ("seq", "batch"), axis=0, tiled=True),
        lax.all_gather(shards[12], ("seq", "batch"), axis=0, tiled=True),
        lax.all_gather(shards[13], ("seq", "batch"), axis=0, tiled=True),
        lax.all_gather(shards[14], ("seq", "batch"), axis=0, tiled=True),
    )
    (
        ga_full,
        sa_full,
        wq_full,
        bq_full,
        wk_full,
        wv_full,
        bv_full,
        wo_full,
        bo_full,
        gb_full,
        sb_full,
        wu_full,
        bu_full,
        wd_full,
        bd_full,
    ) = gathered
    hidden = tokens[0].astype(jnp.float32)
    local_rows = hidden.shape[0]
    width = hidden.shape[1]
    heads = width // HD
    prefix = prefix_len[0]
    start_row = lax.axis_index("seq") * local_rows
    last_row = start_row + local_rows - 1
    length = local_rows * lax.axis_size("seq")
    block_rows = min(512, length)
    block_count = length // block_rows
    row_ids = start_row + jnp.arange(local_rows, dtype=jnp.int32)
    block_ids = jnp.arange(block_count, dtype=jnp.int32)
    normed_one, factor_one = normalize(hidden)
    norm_one = (normed_one * ga_full.astype(jnp.float32) + sa_full.astype(jnp.float32)).astype(
        jnp.bfloat16
    )
    q_low = (
        jnp.dot(norm_one, wq_full, preferred_element_type=jnp.float32) + bq_full.astype(jnp.float32)
    ).astype(jnp.bfloat16)
    k_low = jnp.dot(norm_one, wk_full, preferred_element_type=jnp.float32).astype(jnp.bfloat16)
    v_low = (
        jnp.dot(norm_one, wv_full, preferred_element_type=jnp.float32) + bv_full.astype(jnp.float32)
    ).astype(jnp.bfloat16)
    k_all, v_all = (
        lax.all_gather(k_low, "seq", axis=0, tiled=True),
        lax.all_gather(v_low, "seq", axis=0, tiled=True),
    )
    q_heads = q_low.reshape(local_rows, heads, HD)

    def lse_step(state, item):
        k_part, index = item
        col_ids = index * block_rows + jnp.arange(block_rows, dtype=jnp.int32)

        def lse_update(current):
            scores, allowed = pair_scores(q_heads, k_part, row_ids, col_ids, prefix)
            new_top = jnp.maximum(current[0], jnp.max(scores, axis=-1))
            total = current[1] * jnp.exp(current[0] - new_top) + jnp.sum(
                jnp.exp(scores - new_top[:, :, None]), axis=-1
            )
            return (new_top, total)

        needed = (index * block_rows <= last_row) | (index * block_rows < prefix)
        return (lax.cond(needed, lse_update, lambda current: current, state), None)

    k_blocks = k_all.reshape(block_count, block_rows, heads, HD)
    v_blocks = v_all.reshape(block_count, block_rows, heads, HD)
    lse_start = (
        jnp.full((heads, local_rows), -1e30, jnp.float32),
        jnp.zeros((heads, local_rows), jnp.float32),
    )
    (top_all, total_all), _ = lax.scan(lse_step, lse_start, (k_blocks, block_ids))
    lse = top_all + jnp.log(total_all)

    def out_step(acc, item):
        k_part, v_part, index = item
        col_ids = index * block_rows + jnp.arange(block_rows, dtype=jnp.int32)

        def out_update(current):
            scores, allowed = pair_scores(q_heads, k_part, row_ids, col_ids, prefix)
            attn_prob = jnp.where(allowed[None], jnp.exp(scores - lse[:, :, None]), 0.0).astype(
                jnp.bfloat16
            )
            return current + jnp.einsum(
                "hqk,khd->qhd", attn_prob, v_part, preferred_element_type=jnp.float32
            )

        needed = (index * block_rows <= last_row) | (index * block_rows < prefix)
        return (lax.cond(needed, out_update, lambda current: current, acc), None)

    ctx_acc, _ = lax.scan(
        out_step, jnp.zeros((local_rows, heads, HD), jnp.float32), (k_blocks, v_blocks, block_ids)
    )
    ctx_low = ctx_acc.reshape(local_rows, width).astype(jnp.bfloat16)
    middle = (
        hidden
        + jnp.dot(ctx_low, wo_full, preferred_element_type=jnp.float32)
        + bo_full.astype(jnp.float32)
    )
    normed_two, factor_two = normalize(middle)
    norm_two = (normed_two * gb_full.astype(jnp.float32) + sb_full.astype(jnp.float32)).astype(
        jnp.bfloat16
    )
    pre_act = jnp.dot(norm_two, wu_full, preferred_element_type=jnp.float32) + bu_full.astype(
        jnp.float32
    )
    cdf_part = 0.5 * (1.0 + jax.scipy.special.erf(pre_act * 0.7071067811865476))
    act_low = (pre_act * cdf_part).astype(jnp.bfloat16)
    layer_out = (
        middle
        + jnp.dot(act_low, wd_full, preferred_element_type=jnp.float32)
        + bd_full.astype(jnp.float32)
    ).astype(jnp.bfloat16)
    regathered = (
        lax.all_gather(shards[0], ("seq", "batch"), axis=0, tiled=True),
        lax.all_gather(shards[1], ("seq", "batch"), axis=0, tiled=True),
        lax.all_gather(shards[2], ("seq", "batch"), axis=0, tiled=True),
        lax.all_gather(shards[3], ("seq", "batch"), axis=0, tiled=True),
        lax.all_gather(shards[4], ("seq", "batch"), axis=0, tiled=True),
        lax.all_gather(shards[5], ("seq", "batch"), axis=0, tiled=True),
        lax.all_gather(shards[6], ("seq", "batch"), axis=0, tiled=True),
        lax.all_gather(shards[7], ("seq", "batch"), axis=0, tiled=True),
        lax.all_gather(shards[8], ("seq", "batch"), axis=0, tiled=True),
        lax.all_gather(shards[9], ("seq", "batch"), axis=0, tiled=True),
        lax.all_gather(shards[10], ("seq", "batch"), axis=0, tiled=True),
        lax.all_gather(shards[11], ("seq", "batch"), axis=0, tiled=True),
        lax.all_gather(shards[12], ("seq", "batch"), axis=0, tiled=True),
        lax.all_gather(shards[13], ("seq", "batch"), axis=0, tiled=True),
        lax.all_gather(shards[14], ("seq", "batch"), axis=0, tiled=True),
    )
    (
        ga_back,
        sa_back,
        wq_back,
        bq_back,
        wk_back,
        wv_back,
        bv_back,
        wo_back,
        bo_back,
        gb_back,
        sb_back,
        wu_back,
        bu_back,
        wd_back,
        bd_back,
    ) = regathered
    d_out = cotangent[0]
    grad_wd = over_rows(act_low, d_out)
    grad_bd = jnp.sum(d_out.astype(jnp.float32), axis=0)
    d_act = over_cols(d_out, wd_back)
    slope = cdf_part + pre_act * jnp.exp(-0.5 * pre_act * pre_act) * 0.3989422804014327
    d_pre = (d_act * slope).astype(jnp.bfloat16)
    grad_wu = over_rows(norm_two, d_pre)
    grad_bu = jnp.sum(d_pre.astype(jnp.float32), axis=0)
    d_norm_two = over_cols(d_pre, wu_back)
    d_mid_norm, grad_gb, grad_sb = norm_backward(d_norm_two, normed_two, factor_two, gb_back)
    d_middle = d_out.astype(jnp.float32) + d_mid_norm
    d_branch = d_middle.astype(jnp.bfloat16)
    grad_wo = over_rows(ctx_low, d_branch)
    grad_bo = jnp.sum(d_branch.astype(jnp.float32), axis=0)
    d_ctx = over_cols(d_branch, wo_back).astype(jnp.bfloat16)
    do_heads = d_ctx.reshape(local_rows, heads, HD)
    delta = jnp.sum(d_ctx.astype(jnp.float32).reshape(local_rows, heads, HD) * ctx_acc, axis=-1).T
    k_back, v_back = (k_blocks, v_blocks)
    zero_heads = jnp.zeros((local_rows, heads, HD), jnp.float32)

    def grad_step(acc, item):
        k_part, v_part, index = item
        col_ids = index * block_rows + jnp.arange(block_rows, dtype=jnp.int32)

        def work(current):
            prob_low, d_score = grad_terms(
                q_heads, do_heads, lse, delta, k_part, v_part, row_ids, col_ids, prefix
            )
            current = current + 0.125 * jnp.einsum(
                "hqk,khd->qhd", d_score, k_part, preferred_element_type=jnp.float32
            )
            d_key = 0.125 * jnp.einsum(
                "hqk,qhd->khd", d_score, q_heads, preferred_element_type=jnp.float32
            )
            d_value = jnp.einsum(
                "hqk,qhd->khd", prob_low, do_heads, preferred_element_type=jnp.float32
            )
            return (current, (d_key, d_value))

        def skip(current):
            empty = jnp.zeros((block_rows, heads, HD), jnp.float32)
            return (current, (empty, empty))

        needed = (index * block_rows <= last_row) | (index * block_rows < prefix)
        return lax.cond(needed, work, skip, acc)

    dq_acc, (dk_blocks, dv_blocks) = lax.scan(grad_step, zero_heads, (k_back, v_back, block_ids))
    dk_local, dv_local = (
        lax.psum_scatter(
            dk_blocks.reshape(length, width).astype(jnp.bfloat16),
            "seq",
            scatter_dimension=0,
            tiled=True,
        ).astype(jnp.float32),
        lax.psum_scatter(
            dv_blocks.reshape(length, width).astype(jnp.bfloat16),
            "seq",
            scatter_dimension=0,
            tiled=True,
        ).astype(jnp.float32),
    )
    dq_low = dq_acc.reshape(local_rows, width).astype(jnp.bfloat16)
    dk_low = dk_local.astype(jnp.bfloat16)
    dv_low = dv_local.astype(jnp.bfloat16)
    grad_wq = over_rows(norm_one, dq_low)
    grad_bq = jnp.sum(dq_low.astype(jnp.float32), axis=0)
    grad_wk = over_rows(norm_one, dk_low)
    grad_wv = over_rows(norm_one, dv_low)
    grad_bv = jnp.sum(dv_low.astype(jnp.float32), axis=0)
    d_norm_one = (
        over_cols(dq_low, wq_back) + over_cols(dk_low, wk_back) + over_cols(dv_low, wv_back)
    )
    d_in_norm, grad_ga, grad_sa = norm_backward(d_norm_one, normed_one, factor_one, ga_back)
    grad_tokens = d_middle + d_in_norm
    summed = (
        lax.psum_scatter(grad_ga, ("seq", "batch"), scatter_dimension=0, tiled=True),
        lax.psum_scatter(grad_sa, ("seq", "batch"), scatter_dimension=0, tiled=True),
        lax.psum_scatter(grad_wq, ("seq", "batch"), scatter_dimension=0, tiled=True),
        lax.psum_scatter(grad_bq, ("seq", "batch"), scatter_dimension=0, tiled=True),
        lax.psum_scatter(grad_wk, ("seq", "batch"), scatter_dimension=0, tiled=True),
        lax.psum_scatter(grad_wv, ("seq", "batch"), scatter_dimension=0, tiled=True),
        lax.psum_scatter(grad_bv, ("seq", "batch"), scatter_dimension=0, tiled=True),
        lax.psum_scatter(grad_wo, ("seq", "batch"), scatter_dimension=0, tiled=True),
        lax.psum_scatter(grad_bo, ("seq", "batch"), scatter_dimension=0, tiled=True),
        lax.psum_scatter(grad_gb, ("seq", "batch"), scatter_dimension=0, tiled=True),
        lax.psum_scatter(grad_sb, ("seq", "batch"), scatter_dimension=0, tiled=True),
        lax.psum_scatter(grad_wu, ("seq", "batch"), scatter_dimension=0, tiled=True),
        lax.psum_scatter(grad_bu, ("seq", "batch"), scatter_dimension=0, tiled=True),
        lax.psum_scatter(grad_wd, ("seq", "batch"), scatter_dimension=0, tiled=True),
        lax.psum_scatter(grad_bd, ("seq", "batch"), scatter_dimension=0, tiled=True),
    )
    return (
        layer_out[None],
        grad_tokens[None],
        summed[0],
        summed[1],
        summed[2],
        summed[3],
        summed[4],
        summed[5],
        summed[6],
        summed[7],
        summed[8],
        summed[9],
        summed[10],
        summed[11],
        summed[12],
        summed[13],
        summed[14],
    )


def solution(mesh):
    placed = (
        P("batch", "seq", None),
        P("batch", "seq", None),
        P("batch"),
        P(("seq", "batch")),
        P(("seq", "batch")),
        P(("seq", "batch"), None),
        P(("seq", "batch")),
        P(("seq", "batch"), None),
        P(("seq", "batch"), None),
        P(("seq", "batch")),
        P(("seq", "batch"), None),
        P(("seq", "batch")),
        P(("seq", "batch")),
        P(("seq", "batch")),
        P(("seq", "batch"), None),
        P(("seq", "batch")),
        P(("seq", "batch"), None),
        P(("seq", "batch")),
    )
    return jax.shard_map(
        body,
        mesh=mesh,
        in_specs=placed,
        out_specs=(
            P("batch", "seq", None),
            P("batch", "seq", None),
            P(("seq", "batch")),
            P(("seq", "batch")),
            P(("seq", "batch"), None),
            P(("seq", "batch")),
            P(("seq", "batch"), None),
            P(("seq", "batch"), None),
            P(("seq", "batch")),
            P(("seq", "batch"), None),
            P(("seq", "batch")),
            P(("seq", "batch")),
            P(("seq", "batch")),
            P(("seq", "batch"), None),
            P(("seq", "batch")),
            P(("seq", "batch"), None),
            P(("seq", "batch")),
        ),
        check_vma=False,
    )
```

profile of v0, /device:TPU:0, one launch (start us, length us, event | category | flops | bytes accessed | tf_op | source)
XLA Modules:
  0.0 1545.5 jit_solution(5383057277159908306)
XLA Ops:
  17.0 42.6 %all-reduce.19 = (bf16[768]{0:T(1024)(128)(2,1)S(1)}, bf16[768]{0:T(1024)(128)(2,1)S(1)}, bf16[768]{0:T(1024)(128)(2,1)S(1)}, bf16[768]{0:T(1024)(128)(2,1)S(1)}...) all-reduce(bf16[768]{0:T(1024)(128)(2,1)S(1)} %dynamic-update-slice, ...), channel_id=1, replica_groups=mesh['seq'=16,'batch'=2] {'seq','batch'}, use_global_device_ids=true, to_apply=%add.1 | all-reduce | flops 9216 | bytes 36864
  61.9 6.2 all-gather.15.cloned.1.call-done
  70.6 53.2 %all-gather.9.cloned.1.call-done = bf16[768,768]{1,0:T(8,128)(2,1)} async-done(((bf16[24,768]{1,0:T(8,128)(2,1)}), bf16[768,768]{1,0:T(8,128)(2,1)}) %all-gather.9.cloned.1.call-update) | async-done | bytes 1179664 | tf_op jit(solution)/shard_map/all_gather | solution.py:99
  130.1 49.6 %all-gather.13.cloned.1.call-done = bf16[768,768]{1,0:T(8,128)(2,1)} async-done(((bf16[24,768]{1,0:T(8,128)(2,1)}), bf16[768,768]{1,0:T(8,128)(2,1)}) %all-gather.13.cloned.1.call-update) | async-done | bytes 1179664 | tf_op jit(solution)/shard_map/all_gather | solution.py:97
  181.5 68.5 %all-gather.17.cloned.1.call-done = bf16[2048,768]{1,0:T(8,128)(2,1)} async-done(((bf16[128,768]{1,0:T(8,128)(2,1)}), bf16[2048,768]{1,0:T(8,128)(2,1)}) %all-gather.17.cloned.1.call-update) | async-done | bytes 3145744 | tf_op jit(solution)/shard_map/all_gather | solution.py:153
  261.4 58.4 %all-gather.11.cloned.1.call-done = bf16[2048,768]{1,0:T(8,128)(2,1)} async-done(((bf16[128,768]{1,0:T(8,128)(2,1)}), bf16[2048,768]{1,0:T(8,128)(2,1)}) %all-gather.11.cloned.1.call-update) | async-done | bytes 3145744 | tf_op jit(solution)/shard_map/all_gather | solution.py:152
  331.4 11.3 while.45
  342.8 11.4 while.46
  354.3 20.9 %all-gather.19.cloned.1.call-done = bf16[768,768]{1,0:T(8,128)(2,1)} async-done(((bf16[24,768]{1,0:T(8,128)(2,1)}), bf16[768,768]{1,0:T(8,128)(2,1)}) %all-gather.19.cloned.1.call-update) | async-done | bytes 1179664 | tf_op jit(solution)/shard_map/all_gather | solution.py:102
  377.2 63.5 %all-gather.21.cloned.1.call-done = bf16[768,3072]{1,0:T(8,128)(2,1)} async-done(((bf16[24,3072]{1,0:T(8,128)(2,1)}), bf16[768,3072]{1,0:T(8,128)(2,1)}) %all-gather.21.cloned.1.call-update) | async-done | bytes 4718608 | tf_op jit(solution)/shard_map/all_gather | solution.py:106
  444.0 62.2 %all-gather.23.cloned.1.call-done = bf16[3072,768]{1,0:T(8,128)(2,1)} async-done(((bf16[96,768]{1,0:T(8,128)(2,1)}), bf16[3072,768]{1,0:T(8,128)(2,1)}) %all-gather.23.cloned.1.call-update) | async-done | bytes 4718608 | tf_op jit(solution)/shard_map/all_gather | solution.py:108
  515.0 22.2 %while.47 = (s32[]{:T(128)}, f32[128,12,64]{0,2,1:T(8,128)S(1)}, bf16[4,512,12,64]{1,3,2,0:T(8,128)(2,1)}, bf16[4,512,12,64]{1,3,2,0:T(8,128)(2,1)}, s32[4]{0:T(...) while((s32[]{:T(128)}, f32[128,12,64]{0,2,1:T(8,128)S(1)}, ...), condition=%wide.region_20.21_spmd.clone, body=%wide.region_17.20_spmd.clone.sunk | while | flops 513868928 | bytes 23059832 | solution.py:300
  517.1 8.6 conditional.11
  566.1 137.8 %reduce-scatter.27.cloned.1.call-done = bf16[128,768]{1,0:T(8,128)(2,1)} async-done(((bf16[2048,768]{1,0:T(8,128)(2,1)}), bf16[128,768]{1,0:T(8,128)(2,1)}) %reduce-scatter.27.cloned.1.call-update) | async-done | bytes 196624
  707.0 131.5 %reduce-scatter.25.cloned.1.call-done = bf16[128,768]{1,0:T(8,128)(2,1)} async-done(((bf16[2048,768]{1,0:T(8,128)(2,1)}), bf16[128,768]{1,0:T(8,128)(2,1)}) %reduce-scatter.25.cloned.1.call-update) | async-done | bytes 196624
  841.5 5.1 fusion.93
  847.3 6.3 fusion.103
  864.4 41.3 %all-reduce.18 = (f32[768]{0:T(1024)S(1)}, f32[768]{0:T(1024)S(1)}, f32[768]{0:T(1024)S(1)}, f32[768]{0:T(1024)S(1)}, f32[768]{0:T(1024)S(1)}, /*index=5*/f32[76...) all-reduce(f32[768]{0:T(1024)S(1)} %get-tuple-element.633, ...), channel_id=4, replica_groups=mesh['seq'=16,'batch'=2] {'seq','batch'}, use_global_device_ids=true, to_apply=%region_26.27.clone | all-reduce | flops 9216 | bytes 73728
  911.9 30.7 %reduce-scatter.19.cloned.1.call-done = f32[24,768]{1,0:T(8,128)} async-done(((f32[768,768]{1,0:T(8,128)}), f32[24,768]{1,0:T(8,128)}) %reduce-scatter.19.cloned.1.call-update) | async-done | bytes 73744 | tf_op jit(solution)/shard_map/reduce_scatter | solution.py:336
  942.6 104.6 %reduce-scatter.13.cloned.1.call-done = f32[24,768]{1,0:T(8,128)} async-done(((f32[768,768]{1,0:T(8,128)}), f32[24,768]{1,0:T(8,128)}) %reduce-scatter.13.cloned.1.call-update) | async-done | bytes 73744 | tf_op jit(solution)/shard_map/reduce_scatter | solution.py:331
  1047.3 103.9 %reduce-scatter.17.cloned.1.call-done = f32[24,768]{1,0:T(8,128)} async-done(((f32[768,768]{1,0:T(8,128)}), f32[24,768]{1,0:T(8,128)}) %reduce-scatter.17.cloned.1.call-update) | async-done | bytes 73744 | tf_op jit(solution)/shard_map/reduce_scatter | solution.py:334
  1151.2 104.6 %reduce-scatter.15.cloned.1.call-done = f32[24,768]{1,0:T(8,128)} async-done(((f32[768,768]{1,0:T(8,128)}), f32[24,768]{1,0:T(8,128)}) %reduce-scatter.15.cloned.1.call-update) | async-done | bytes 73744 | tf_op jit(solution)/shard_map/reduce_scatter | solution.py:333
  1255.8 141.0 %reduce-scatter.23.cloned.1.call-done = f32[96,768]{1,0:T(8,128)} async-done(((f32[3072,768]{1,0:T(8,128)}), f32[96,768]{1,0:T(8,128)}) %reduce-scatter.23.cloned.1.call-update) | async-done | bytes 294928 | tf_op jit(solution)/shard_map/reduce_scatter | solution.py:342
  1396.8 141.9 %reduce-scatter.21.cloned.1.call-done = f32[24,3072]{1,0:T(8,128)} async-done(((f32[768,3072]{1,0:T(8,128)}), f32[24,3072]{1,0:T(8,128)}) %reduce-scatter.21.cloned.1.call-update) | async-done | bytes 294928 | tf_op jit(solution)/shard_map/reduce_scatter | solution.py:340
  (271 shorter events, 147.8 us)
Async XLA Ops:
  7.2 172.5 %copy-start.3 = (bf16[1,128,768]{2,1,0:T(8,128)(2,1)S(1)}, bf16[1,128,768]{2,1,0:T(8,128)(2,1)}, u32[]{:S(2)}) copy-start(bf16[1,128,768]{2,1,0:T(8,128)(2,1)} %param.30) | copy-start | bytes 589828
  7.2 60.9 %all-gather.15.cloned.1.call-start = ((), (), s32[]{:S(2)}) async-start(), calls=%async_computation.11 | async-start | bytes 1216512 | tf_op jit(solution)/shard_map/all_gather | solution.py:100
  7.9 115.9 %all-gather.9.cloned.1.call-start = ((), (), s32[]{:S(2)}) async-start(), calls=%async_computation.8 | async-start | bytes 1216512 | tf_op jit(solution)/shard_map/all_gather | solution.py:99
  8.7 171.0 %all-gather.13.cloned.1.call-start = ((), (), s32[]{:S(2)}) async-start(), calls=%async_computation.10 | async-start | bytes 1216512 | tf_op jit(solution)/shard_map/all_gather | solution.py:97
  9.4 240.6 %all-gather.17.cloned.1.call-start = ((), (), s32[]{:S(2)}) async-start(), calls=%async_computation.12 | async-start | bytes 3342336 | tf_op jit(solution)/shard_map/all_gather | solution.py:153
  60.7 119.0 %copy-start.16 = (f32[128]{0:T(128)}, f32[128]{0:T(128)S(1)}, u32[]{:S(2)}) copy-start(f32[128]{0:T(128)S(1)} %broadcast_multiply_fusion.5) | copy-start | bytes 1540
  61.9 117.8 %copy-start.27 = (f32[128]{0:T(128)}, f32[128]{0:T(128)S(1)}, u32[]{:S(2)}) copy-start(f32[128]{0:T(128)S(1)} %add_rsqrt_fusion.1) | copy-start | bytes 1540
  70.5 249.3 %all-gather.11.cloned.1.call-start = ((), (), s32[]{:S(2)}) async-start(), calls=%async_computation.9 | async-start | bytes 3342336 | tf_op jit(solution)/shard_map/all_gather | solution.py:152
  126.3 249.0 %all-gather.19.cloned.1.call-start = ((), (), s32[]{:S(2)}) async-start(), calls=%async_computation.13 | async-start | bytes 1216512 | tf_op jit(solution)/shard_map/all_gather | solution.py:102
  126.8 313.9 %all-gather.21.cloned.1.call-start = ((), (), s32[]{:S(2)}) async-start(), calls=%async_computation.14 | async-start | bytes 4866048 | tf_op jit(solution)/shard_map/all_gather | solution.py:106
  127.6 378.5 %all-gather.23.cloned.1.call-start = ((), (), s32[]{:S(2)}) async-start(), calls=%async_computation.15 | async-start | bytes 4866048 | tf_op jit(solution)/shard_map/all_gather | solution.py:108
  128.3 575.6 %reduce-scatter.27.cloned.1.call-start = ((), (), s32[]{:S(2)}) async-start(), calls=%async_computation.23 | async-start | bytes 3342336
  342.8 97.9 %copy-start.12 = (f32[3072]{0:T(1024)S(1)}, f32[3072]{0:T(1024)}, u32[]{:S(2)}) copy-start(f32[3072]{0:T(1024)} %convert_element_type.159) | copy-start | bytes 36868
  354.3 89.6 %copy-start.6 = (bf16[128,12,64]{0,2,1:T(8,128)(2,1)}, bf16[128,12,64]{0,2,1:T(8,128)(2,1)S(1)}, u32[]{:S(2)}) copy-start(bf16[128,12,64]{0,2,1:T(8,128)(2,1)S(1)} %convert_element_type.153) | copy-start | bytes 589828
  443.9 67.1 %copy-start = (f32[128,3072]{1,0:T(8,128)}, f32[128,3072]{1,0:T(8,128)S(1)}, u32[]{:S(2)}) copy-start(f32[128,3072]{1,0:T(8,128)S(1)} %convolution_add_fusion) | copy-start | bytes 4718596
  549.0 289.6 %reduce-scatter.25.cloned.1.call-start = ((), (), s32[]{:S(2)}) async-start(), calls=%async_computation.22 | async-start | bytes 3342336
  560.9 381.7 %reduce-scatter.19.cloned.1.call-start = ((), (), s32[]{:S(2)}) async-start(), calls=%async_computation.19 | async-start | bytes 2433024 | tf_op jit(solution)/shard_map/reduce_scatter | solution.py:336
  563.7 483.6 %reduce-scatter.13.cloned.1.call-start = ((), (), s32[]{:S(2)}) async-start(), calls=%async_computation.16 | async-start | bytes 2433024 | tf_op jit(solution)/shard_map/reduce_scatter | solution.py:331
  566.0 585.2 %reduce-scatter.17.cloned.1.call-start = ((), (), s32[]{:S(2)}) async-start(), calls=%async_computation.18 | async-start | bytes 2433024 | tf_op jit(solution)/shard_map/reduce_scatter | solution.py:334
  707.0 134.5 %copy-start.1 = (f32[128,3072]{1,0:T(8,128)S(1)}, f32[128,3072]{1,0:T(8,128)}, u32[]{:S(2)}) copy-start(f32[128,3072]{1,0:T(8,128)} %copy-done) | copy-start | bytes 4718596
  707.0 134.5 %copy-start.10 = (bf16[1,128,768]{2,1,0:T(8,128)(2,1)S(1)}, bf16[1,128,768]{2,1,0:T(8,128)(2,1)}, u32[]{:S(2)}) copy-start(bf16[1,128,768]{2,1,0:T(8,128)(2,1)} %param.31) | copy-start | bytes 589828
  707.0 548.9 %reduce-scatter.15.cloned.1.call-start = ((), (), s32[]{:S(2)}) async-start(), calls=%async_computation.17 | async-start | bytes 2433024 | tf_op jit(solution)/shard_map/reduce_scatter | solution.py:333
  841.4 555.4 %reduce-scatter.23.cloned.1.call-start = ((), (), s32[]{:S(2)}) async-start(), calls=%async_computation.21 | async-start | bytes 9732096 | tf_op jit(solution)/shard_map/reduce_scatter | solution.py:342
  846.6 692.1 %reduce-scatter.21.cloned.1.call-start = ((), (), s32[]{:S(2)}) async-start(), calls=%async_computation.20 | async-start | bytes 9732096 | tf_op jit(solution)/shard_map/reduce_scatter | solution.py:340
  (26 other events, 263.3 us)
Sparse Core Ops, SparseCore 0:
  10.9 57.0 all-gather.14
  71.0 52.7 all-gather.8
  126.7 52.9 all-gather.12
  182.9 67.0 all-gather.16
  253.2 66.6 all-gather.10
  322.6 52.5 all-gather.18
  378.1 62.5 all-gather.20
  443.6 62.4 all-gather.22
  549.1 154.7 reduce-scatter.26
  708.7 129.7 reduce-scatter.24
  844.4 98.2 reduce-scatter.18
  949.2 98.0 reduce-scatter.12
  1053.1 98.0 reduce-scatter.16
  1157.8 98.0 reduce-scatter.14
  1262.2 134.5 reduce-scatter.22
  1404.1 134.4 reduce-scatter.20
where the time goes:
time: 1550 us
  waiting for transfers between devices  1280 us (83%)
  blocking collectives  84 us (5%)
  local copies, waits for them, and re-layouts  74.9 us (5%)
  matrix products  62.4 us (4%)
  loops' own time  16.7 us (1%)
    unnamed x18, waiting for transfers between devices  273 us
    reduce_scatter x1, waiting for transfers between devices, body(): lax.psum_scatter(grad_wu, ('seq', 'batch'), scatter_dimension=0, tiled=True)  142 us
    reduce_scatter x1, waiting for transfers between devices, body(): lax.psum_scatter(grad_wd, ('seq', 'batch'), scatter_dimension=0, tiled=True)  141 us
    reduce_scatter x1, waiting for transfers between devices, body(): lax.psum_scatter(grad_wk, ('seq', 'batch'), scatter_dimension=0, tiled=True)  105 us
    reduce_scatter x1, waiting for transfers between devices, body(): lax.psum_scatter(grad_wq, ('seq', 'batch'), scatter_dimension=0, tiled=True)  105 us
    reduce_scatter x1, waiting for transfers between devices, body(): lax.psum_scatter(grad_wv, ('seq', 'batch'), scatter_dimension=0, tiled=True)  104 us
    unnamed x2, blocking collectives  84 us
    all_gather x1, waiting for transfers between devices, body(): lax.all_gather(v_low, 'seq', axis=0, tiled=True)  68.5 us
  transfers between devices with their start and end apart: 16, of which 16 were waited for; matrix products, arithmetic and copies ran while one was open for 7% of the time, Pallas kernels for 0%

commit v1 on v0

--- a/solution.py
+++ b/solution.py
@@ -5,6 +5,28 @@
 
 HD = 64
 EPS = 1e-05
+
+
+def joined_along(blocks, dim):
+    blocks = jnp.moveaxis(blocks, 0, dim)
+    shape = blocks.shape
+    return blocks.reshape(*shape[:dim], shape[dim] * shape[dim + 1], *shape[dim + 2 :])
+
+
+def collect(x, axis, dim):
+    size = lax.axis_size(axis)
+    pairs = [(i, (i + 1) % size) for i in range(size)]
+    back = [(b, a) for a, b in pairs]
+    lower, upper = ([], [])
+    for step in range(size - 1):
+        if step % 2 == 0:
+            lower.append(lax.ppermute(lower[-1] if lower else x, axis, pairs))
+        else:
+            upper.append(lax.ppermute(upper[-1] if upper else x, axis, back))
+    pieces = jnp.stack([*lower[::-1], x, *upper])
+    shift = lax.axis_index(axis) - len(lower)
+    pieces = pieces[(jnp.arange(size) - shift) % size]
+    return joined_along(pieces, dim)
 
 
 def normalize(values):
@@ -148,10 +170,7 @@
     v_low = (
         jnp.dot(norm_one, wv_full, preferred_element_type=jnp.float32) + bv_full.astype(jnp.float32)
     ).astype(jnp.bfloat16)
-    k_all, v_all = (
-        lax.all_gather(k_low, "seq", axis=0, tiled=True),
-        lax.all_gather(v_low, "seq", axis=0, tiled=True),
-    )
+    k_all, v_all = (collect(k_low, "seq", 0), lax.all_gather(v_low, "seq", axis=0, tiled=True))
     q_heads = q_low.reshape(local_rows, heads, HD)
 
     def lse_step(state, item):

time: 1550 us -> 1500 us (0.968)
  waiting for transfers between devices: 1280 us -> 1170 us
  starting transfers between devices: 1.11 us -> 45.9 us
    all_gather x1 -> x0, waiting for transfers between devices: 58.4 us -> none  [body(): lax.all_gather(k_low, 'seq', axis=0, tiled=True)]
    all_gather x1, waiting for transfers between devices: 68.5 us -> 11.4 us  [body(): lax.all_gather(v_low, 'seq', axis=0, tiled=True)]
    all_gather x1, waiting for transfers between devices: 49.6 us -> 0.01 us  [body(): lax.all_gather(shards[2], ('seq', 'batch'), axis=0, tiled=True)]
    ppermute x0 -> x15, starting transfers between devices: none -> 45.3 us  [the longest x7 30.9 us: collect(): upper.append(lax.ppermute(upper[-1] if upper else x, axis, back))]
    ppermute x0 -> x15, waiting for transfers between devices: none -> 41.2 us  [the longest x8 41.2 us: collect(): lower.append(lax.ppermute(lower[-1] if lower else x, axis, pairs))]
    unnamed x100 -> x115, local copies, waits for them, and re-layouts: 38.7 us -> 47.2 us
    unnamed x18 -> x17, waiting for transfers between devices: 273 us -> 273 us
  transfers between devices with their start and end apart: 16 -> 30, of which waited for: 16 -> 22; matrix products, arithmetic and copies ran while one was open for 7% -> 8% of each run, Pallas kernels for 0% -> 0%
where the time goes in v1:
time: 1500 us; the launch traced here: 1490 us
  waiting for transfers between devices  1170 us (78%)
  local copies, waits for them, and re-layouts  87.1 us (6%)
  blocking collectives  83.8 us (6%)
  matrix products  61.7 us (4%)
  starting transfers between devices  45.9 us (3%)
  loops' own time  16.7 us (1%)
    unnamed x17, waiting for transfers between devices  273 us
    reduce_scatter x1, waiting for transfers between devices, body(): lax.psum_scatter(grad_wu, ('seq', 'batch'), scatter_dimension=0, tiled=True)  142 us
    reduce_scatter x1, waiting for transfers between devices, body(): lax.psum_scatter(grad_wd, ('seq', 'batch'), scatter_dimension=0, tiled=True)  141 us
    reduce_scatter x1, waiting for transfers between devices, body(): lax.psum_scatter(grad_wq, ('seq', 'batch'), scatter_dimension=0, tiled=True)  105 us
    reduce_scatter x1, waiting for transfers between devices, body(): lax.psum_scatter(grad_wk, ('seq', 'batch'), scatter_dimension=0, tiled=True)  105 us
    reduce_scatter x1, waiting for transfers between devices, body(): lax.psum_scatter(grad_wv, ('seq', 'batch'), scatter_dimension=0, tiled=True)  104 us
    unnamed x2, blocking collectives  83.8 us
    all_gather x1, waiting for transfers between devices, body(): lax.all_gather(shards[11], ('seq', 'batch'), axis=0, tiled=True)  63.4 us
  transfers between devices with their start and end apart: 30, of which 22 were waited for; matrix products, arithmetic and copies ran while one was open for 8% of the time, Pallas kernels for 0%

profile of v1, /device:TPU:0, one launch (start us, length us, event | category | flops | bytes accessed | tf_op | source)
XLA Modules:
  0.0 1488.3 jit_solution(7233281467565956108)
XLA Ops:
  17.0 42.6 %all-reduce.19 = (bf16[768]{0:T(1024)(128)(2,1)S(1)}, bf16[768]{0:T(1024)(128)(2,1)S(1)}, bf16[768]{0:T(1024)(128)(2,1)S(1)}, bf16[768]{0:T(1024)(128)(2,1)S(1)}...) all-reduce(bf16[768]{0:T(1024)(128)(2,1)S(1)} %dynamic-update-slice, ...), channel_id=1, replica_groups=mesh['seq'=16,'batch'=2] {'seq','batch'}, use_global_device_ids=true, to_apply=%add.1 | all-reduce | flops 9216 | bytes 36864
  61.8 6.3 all-gather.12.cloned.1.call-done
  72.5 51.3 %all-gather.8.cloned.1.call-done = bf16[768,768]{1,0:T(8,128)(2,1)} async-done(((bf16[24,768]{1,0:T(8,128)(2,1)}), bf16[768,768]{1,0:T(8,128)(2,1)}) %all-gather.8.cloned.1.call-update) | async-done | bytes 1179664 | tf_op jit(solution)/shard_map/all_gather | solution.py:121
  127.1 9.2 collective-permute-done
  175.0 6.2 collective-permute-done.4
  199.0 6.4 collective-permute-done.6
  239.5 11.3 while.45
  251.4 11.4 all-gather.14.cloned.1.call-done
  274.4 11.4 while.46
  285.9 32.2 %all-gather.16.cloned.1.call-done = bf16[768,768]{1,0:T(8,128)(2,1)} async-done(((bf16[24,768]{1,0:T(8,128)(2,1)}), bf16[768,768]{1,0:T(8,128)(2,1)}) %all-gather.16.cloned.1.call-update) | async-done | bytes 1179664 | tf_op jit(solution)/shard_map/all_gather | solution.py:124
  320.0 63.4 %all-gather.18.cloned.1.call-done = bf16[768,3072]{1,0:T(8,128)(2,1)} async-done(((bf16[24,3072]{1,0:T(8,128)(2,1)}), bf16[768,3072]{1,0:T(8,128)(2,1)}) %all-gather.18.cloned.1.call-update) | async-done | bytes 4718608 | tf_op jit(solution)/shard_map/all_gather | solution.py:128
  386.7 62.1 %all-gather.20.cloned.1.call-done = bf16[3072,768]{1,0:T(8,128)(2,1)} async-done(((bf16[96,768]{1,0:T(8,128)(2,1)}), bf16[3072,768]{1,0:T(8,128)(2,1)}) %all-gather.20.cloned.1.call-update) | async-done | bytes 4718608 | tf_op jit(solution)/shard_map/all_gather | solution.py:130
  457.7 22.2 %while.47 = (s32[]{:T(128)}, f32[128,12,64]{0,2,1:T(8,128)S(1)}, bf16[4,512,12,64]{1,3,2,0:T(8,128)(2,1)}, bf16[4,512,12,64]{1,3,2,0:T(8,128)(2,1)}, s32[4]{0:T(...) while((s32[]{:T(128)}, f32[128,12,64]{0,2,1:T(8,128)S(1)}, ...), condition=%wide.region_20.21_spmd.clone, body=%wide.region_17.20_spmd.clone.sunk | while | flops 513868928 | bytes 23059832 | solution.py:319
  459.8 8.6 conditional.11
  508.9 137.5 %reduce-scatter.27.cloned.1.call-done = bf16[128,768]{1,0:T(8,128)(2,1)} async-done(((bf16[2048,768]{1,0:T(8,128)(2,1)}), bf16[128,768]{1,0:T(8,128)(2,1)}) %reduce-scatter.27.cloned.1.call-update) | async-done | bytes 196624
  649.4 131.8 %reduce-scatter.25.cloned.1.call-done = bf16[128,768]{1,0:T(8,128)(2,1)} async-done(((bf16[2048,768]{1,0:T(8,128)(2,1)}), bf16[128,768]{1,0:T(8,128)(2,1)}) %reduce-scatter.25.cloned.1.call-update) | async-done | bytes 196624
  790.0 6.3 fusion.105
  807.1 41.3 %all-reduce.18 = (f32[768]{0:T(1024)S(1)}, f32[768]{0:T(1024)S(1)}, f32[768]{0:T(1024)S(1)}, f32[768]{0:T(1024)S(1)}, f32[768]{0:T(1024)S(1)}, /*index=5*/f32[76...) all-reduce(f32[768]{0:T(1024)S(1)} %get-tuple-element.633, ...), channel_id=4, replica_groups=mesh['seq'=16,'batch'=2] {'seq','batch'}, use_global_device_ids=true, to_apply=%region_26.27.clone | all-reduce | flops 9216 | bytes 73728
  854.6 30.7 %reduce-scatter.19.cloned.1.call-done = f32[24,768]{1,0:T(8,128)} async-done(((f32[768,768]{1,0:T(8,128)}), f32[24,768]{1,0:T(8,128)}) %reduce-scatter.19.cloned.1.call-update) | async-done | bytes 73744 | tf_op jit(solution)/shard_map/reduce_scatter | solution.py:355
  885.2 104.8 %reduce-scatter.13.cloned.1.call-done = f32[24,768]{1,0:T(8,128)} async-done(((f32[768,768]{1,0:T(8,128)}), f32[24,768]{1,0:T(8,128)}) %reduce-scatter.13.cloned.1.call-update) | async-done | bytes 73744 | tf_op jit(solution)/shard_map/reduce_scatter | solution.py:350
  990.0 103.8 %reduce-scatter.17.cloned.1.call-done = f32[24,768]{1,0:T(8,128)} async-done(((f32[768,768]{1,0:T(8,128)}), f32[24,768]{1,0:T(8,128)}) %reduce-scatter.17.cloned.1.call-update) | async-done | bytes 73744 | tf_op jit(solution)/shard_map/reduce_scatter | solution.py:353
  1093.8 104.8 %reduce-scatter.15.cloned.1.call-done = f32[24,768]{1,0:T(8,128)} async-done(((f32[768,768]{1,0:T(8,128)}), f32[24,768]{1,0:T(8,128)}) %reduce-scatter.15.cloned.1.call-update) | async-done | bytes 73744 | tf_op jit(solution)/shard_map/reduce_scatter | solution.py:352
  1198.6 141.0 %reduce-scatter.23.cloned.1.call-done = f32[96,768]{1,0:T(8,128)} async-done(((f32[3072,768]{1,0:T(8,128)}), f32[96,768]{1,0:T(8,128)}) %reduce-scatter.23.cloned.1.call-update) | async-done | bytes 294928 | tf_op jit(solution)/shard_map/reduce_scatter | solution.py:361
  1339.5 142.0 %reduce-scatter.21.cloned.1.call-done = f32[24,3072]{1,0:T(8,128)} async-done(((f32[768,3072]{1,0:T(8,128)}), f32[24,3072]{1,0:T(8,128)}) %reduce-scatter.21.cloned.1.call-update) | async-done | bytes 294928 | tf_op jit(solution)/shard_map/reduce_scatter | solution.py:359
  (317 shorter events, 229.7 us)
Async XLA Ops:
  7.2 60.9 %all-gather.12.cloned.1.call-start = ((), (), s32[]{:S(2)}) async-start(), calls=%async_computation.10 | async-start | bytes 1216512 | tf_op jit(solution)/shard_map/all_gather | solution.py:122
  7.9 115.9 %all-gather.8.cloned.1.call-start = ((), (), s32[]{:S(2)}) async-start(), calls=%async_computation.8 | async-start | bytes 1216512 | tf_op jit(solution)/shard_map/all_gather | solution.py:121
  8.7 199.2 %all-gather.10.cloned.1.call-start = ((), (), s32[]{:S(2)}) async-start(), calls=%async_computation.9 | async-start | bytes 1216512 | tf_op jit(solution)/shard_map/all_gather | solution.py:119
  9.4 253.3 %all-gather.14.cloned.1.call-start = ((), (), s32[]{:S(2)}) async-start(), calls=%async_computation.11 | async-start | bytes 3342336 | tf_op jit(solution)/shard_map/all_gather | solution.py:173
  70.5 247.5 %all-gather.16.cloned.1.call-start = ((), (), s32[]{:S(2)}) async-start(), calls=%async_computation.12 | async-start | bytes 1216512 | tf_op jit(solution)/shard_map/all_gather | solution.py:124
  71.1 312.3 %all-gather.18.cloned.1.call-start = ((), (), s32[]{:S(2)}) async-start(), calls=%async_computation.13 | async-start | bytes 4866048 | tf_op jit(solution)/shard_map/all_gather | solution.py:128
  71.7 377.1 %all-gather.20.cloned.1.call-start = ((), (), s32[]{:S(2)}) async-start(), calls=%async_computation.14 | async-start | bytes 4866048 | tf_op jit(solution)/shard_map/all_gather | solution.py:130
  72.5 573.9 %reduce-scatter.27.cloned.1.call-start = ((), (), s32[]{:S(2)}) async-start(), calls=%async_computation.22 | async-start | bytes 3342336
  147.1 12.3 collective-permute-start.9
  156.8 11.0 collective-permute-start.3
  167.8 13.3 collective-permute-start.4
  170.3 14.6 collective-permute-start.11
  181.2 11.6 collective-permute-start.5
  184.9 11.0 collective-permute-start.12
  192.8 12.6 collective-permute-start.6
  195.9 13.8 collective-permute-start.13
  209.7 16.4 %collective-permute-start.14 = (bf16[128,768]{1,0:T(8,128)(2,1)S(1)}, bf16[128,768]{1,0:T(8,128)(2,1)S(1)}, u32[]{:S(2)}, u32[]{:S(2)}) collective-permute-start(bf16[128,768]{1,0:T(8,128)(2,1)S(1)} %collective-permute-done.13), channel_id=1, source_target_pairs={{2,0},{4,2},{6,4},{8,6},{10,8},{12,10},{14,12},{16,14},{18,16},{20... | collective-permute-start | bytes 589832 | tf_op jit(solution)/shard_map/ppermute | solution.py:25
  491.7 289.5 %reduce-scatter.25.cloned.1.call-start = ((), (), s32[]{:S(2)}) async-start(), calls=%async_computation.21 | async-start | bytes 3342336
  503.7 381.5 %reduce-scatter.19.cloned.1.call-start = ((), (), s32[]{:S(2)}) async-start(), calls=%async_computation.18 | async-start | bytes 2433024 | tf_op jit(solution)/shard_map/reduce_scatter | solution.py:355
  506.5 483.6 %reduce-scatter.13.cloned.1.call-start = ((), (), s32[]{:S(2)}) async-start(), calls=%async_computation.15 | async-start | bytes 2433024 | tf_op jit(solution)/shard_map/reduce_scatter | solution.py:350
  508.8 585.0 %reduce-scatter.17.cloned.1.call-start = ((), (), s32[]{:S(2)}) async-start(), calls=%async_computation.17 | async-start | bytes 2433024 | tf_op jit(solution)/shard_map/reduce_scatter | solution.py:353
  649.4 549.2 %reduce-scatter.15.cloned.1.call-start = ((), (), s32[]{:S(2)}) async-start(), calls=%async_computation.16 | async-start | bytes 2433024 | tf_op jit(solution)/shard_map/reduce_scatter | solution.py:352
  784.2 555.3 %reduce-scatter.23.cloned.1.call-start = ((), (), s32[]{:S(2)}) async-start(), calls=%async_computation.20 | async-start | bytes 9732096 | tf_op jit(solution)/shard_map/reduce_scatter | solution.py:361
  789.4 692.2 %reduce-scatter.21.cloned.1.call-start = ((), (), s32[]{:S(2)}) async-start(), calls=%async_computation.19 | async-start | bytes 9732096 | tf_op jit(solution)/shard_map/reduce_scatter | solution.py:359
  (40 other events, 1361.7 us)
Sparse Core Ops, SparseCore 0:
  10.9 57.0 all-gather.11
  71.0 52.7 all-gather.7
  126.7 60.2 all-gather.9
  190.2 72.4 all-gather.13
  265.5 52.5 all-gather.15
  320.8 62.5 all-gather.17
  386.3 62.4 all-gather.19
  491.8 154.4 reduce-scatter.26
  651.3 129.8 reduce-scatter.24
  787.0 98.2 reduce-scatter.18
  892.0 98.0 reduce-scatter.12
  995.7 97.9 reduce-scatter.16
  1100.5 98.0 reduce-scatter.14
  1204.9 134.5 reduce-scatter.22
  1346.9 134.6 reduce-scatter.20
